TPU v7x, 512 devices: a whole 4x4x16 slice. The times are simulated.
512 devices in a mesh: loop: 32 (over z, y_hi), rep: 4 (over x), feat: 4 (over y_lo, core).
Axes of the slice: x: 4, y: 4 (y_hi: 2, y_lo: 2; y = y_hi * 2 + y_lo), z: 16, core: 2. Of those that a mesh axis runs over, the one named last changes fastest.
Arguments:
- features: bfloat16 [128, 32768], P('feat', 'loop'), may hold values from -6 to 6
- tile_values: bfloat16 [32, 4, 112, 128, 128], P('loop', 'rep'), may hold values from -0.1875 to 0.1875
- tile_coords: int32 [32, 4, 2, 112], P('loop', 'rep'), may hold values from 0 to 7, as said below
- section_counts: int32 [32, 4, 8], P('loop', 'rep'), may hold values from 0 to 64, as said below
- weight_one: bfloat16 [128, 128], replicated, may hold values from -0.5 to 0.5
- weight_two: bfloat16 [128, 128], replicated, may hold values from -0.5 to 0.5
- cotangent: bfloat16 [128, 32768], P(None, ('loop', 'feat')), may hold values from -24 to 24
Outputs:
- grad_one: float32 [128, 128], replicated
- grad_two: float32 [128, 128], replicated
- input_grad: bfloat16 [128, 32768], P('feat', 'loop')
Inputs may be any that keep to these rules, and one draw needn't show every extreme that they name: `tile_coords`: slots of a list are grouped by section in order of sections; the live slots of one section name distinct (row, column) pairs; slots past the list's total count hold 0. `section_counts`: section k of rep index r covers the column block r + 4 * k places below the list's own loop index; sections with r + 4 * k of 32 or more hold 0.
All inputs are finite; a program needn't handle non-finite values.
Results may differ from a plain program's by a relative error of at most 0.029.
Values may be sent and summed in bfloat16 or wider, within the bound.
A program may use at most 64 MiB of HBM per device.

v0:
```python
import math
import jax
import jax.numpy as jnp
from jax import lax
from jax.sharding import PartitionSpec as P

tile_batch = 8


def passed_along(value, axis, steps):
    count = lax.axis_size(axis)
    pairs = [(source, (source + steps) % count) for source in range(count)]
    return lax.ppermute(value, axis, pairs)


def silu_slope(argument):
    sigmoid_value = jax.nn.sigmoid(argument)
    return sigmoid_value * (1.0 + argument * (1.0 - sigmoid_value))


def section_term(source, section_id, layout, transposed, enabled=True):
    tile_set, row_ids, col_ids, starts, filled, panels = layout
    feat_width = source.shape[0]
    tile_side = tile_set.shape[-1]
    slot_total = tile_set.shape[0]
    shaped = source.reshape(feat_width, panels, tile_side)
    first = starts[section_id]
    number = jnp.where(enabled, filled[section_id], 0)
    rounds = (number + tile_batch - 1) // tile_batch
    offsets = jnp.arange(tile_batch, dtype=jnp.int32)
    panel_ids = jnp.arange(panels, dtype=jnp.int32)

    def one_round(round_id, running):
        within = round_id * tile_batch + offsets
        alive_mask = within < number
        slot_ids = jnp.minimum(first + within, slot_total - 1)
        chosen = tile_set[slot_ids]
        if transposed:
            picked = shaped[:, row_ids[slot_ids], :]
            products = jnp.einsum(
                "dba,bac->dbc", picked, chosen, preferred_element_type=jnp.float32
            )
            target = col_ids[slot_ids]
        else:
            picked = shaped[:, col_ids[slot_ids], :]
            products = jnp.einsum(
                "dbc,bac->dba", picked, chosen, preferred_element_type=jnp.float32
            )
            target = row_ids[slot_ids]
        placing = ((target[:, None] == panel_ids[None, :]) & alive_mask[:, None]).astype(
            jnp.float32
        )
        return running + jnp.einsum(
            "dbe,bp->dpe", products, placing, precision=lax.Precision.HIGHEST
        )

    zero_block = jnp.zeros((feat_width, panels, tile_side), jnp.float32)
    return lax.fori_loop(0, rounds, one_round, zero_block).reshape(feat_width, panels * tile_side)


def advance(block, stride):
    return passed_along(block, "loop", stride)


def forward_product(source, layout):
    loop_size = lax.axis_size("loop")
    rep_size = lax.axis_size("rep")
    rep_index = lax.axis_index("rep")
    sections = -(-loop_size // rep_size)
    stride = rep_size % loop_size
    current = source
    for bit in range(rep_size.bit_length() - 1):
        jump = (1 << bit) % loop_size
        moved = passed_along(current, "loop", jump)
        current = jnp.where((rep_index >> bit) % 2 == 1, moved, current)
    running = section_term(current, 0, layout, False)

    def onward(step_id, carry):
        ahead, acc = carry
        ahead = advance(ahead, stride)
        return (ahead, acc + section_term(ahead, step_id, layout, False))

    ahead, running = lax.fori_loop(1, sections, onward, (current, running))
    return running


def transposed_product(source, layout):
    loop_size = lax.axis_size("loop")
    rep_size = lax.axis_size("rep")
    rep_index = lax.axis_index("rep")
    sections = -(-loop_size // rep_size)
    stride = rep_size % loop_size
    running = section_term(source, sections - 1, layout, True)

    def backward(step_id, acc):
        acc = passed_along(acc.astype(jnp.bfloat16), "loop", -stride).astype(acc.dtype)
        return acc + section_term(source, sections - 1 - step_id, layout, True)

    running = lax.fori_loop(1, sections, backward, running)
    for bit in range(rep_size.bit_length() - 1):
        jump = (1 << bit) % loop_size
        moved = passed_along(running.astype(jnp.bfloat16), "loop", -jump).astype(running.dtype)
        running = jnp.where((rep_index >> bit) % 2 == 1, moved, running)
    return running


def to_nodes(partial_value):
    summed = lax.psum(partial_value.astype(jnp.bfloat16), "rep")
    return lax.all_to_all(summed, "feat", split_axis=1, concat_axis=0, tiled=True)


def to_features(node_block):
    return lax.all_to_all(node_block, "feat", split_axis=0, concat_axis=1, tiled=True)


def weight_grad(mixed, slope):
    part_sum = jnp.einsum("dq,eq->de", mixed, slope, preferred_element_type=jnp.float32)
    return lax.psum(part_sum, ("loop", "feat"))


def shards(features, tile_values, tile_coords, section_counts, weight_one, weight_two, cotangent):
    tile_set = tile_values[0, 0]
    row_ids = tile_coords[0, 0, 0]
    col_ids = tile_coords[0, 0, 1]
    filled = section_counts[0, 0]
    starts = jnp.cumsum(filled) - filled
    panels = features.shape[1] // tile_set.shape[-1]
    layout = (tile_set, row_ids, col_ids, starts, filled, panels)
    scale = 1.0 / math.sqrt(features.shape[1] * lax.axis_size("loop"))
    mix_one = to_nodes(forward_product(features, layout))
    z_one = jnp.einsum("de,dq->eq", weight_one, mix_one, preferred_element_type=jnp.float32)
    h_one = jax.nn.silu(z_one).astype(jnp.bfloat16)
    mix_two = to_nodes(forward_product(to_features(h_one), layout))
    z_two = jnp.einsum("de,dq->eq", weight_two, mix_two, preferred_element_type=jnp.float32)
    dz_two = (cotangent * silu_slope(z_two)).astype(jnp.bfloat16)
    grad_two = weight_grad(mix_two, dz_two) * scale
    dm_two = jnp.einsum("de,eq->dq", weight_two, dz_two, preferred_element_type=jnp.float32).astype(
        jnp.bfloat16
    )
    dh_one = to_nodes(transposed_product(to_features(dm_two), layout))
    dz_one = (dh_one * silu_slope(z_one)).astype(jnp.bfloat16)
    grad_one = weight_grad(mix_one, dz_one) * scale
    dm_one = jnp.einsum("de,eq->dq", weight_one, dz_one, preferred_element_type=jnp.float32).astype(
        jnp.bfloat16
    )
    partial_value = transposed_product(to_features(dm_one), layout)
    input_grad = lax.psum(partial_value.astype(jnp.bfloat16), "rep")
    return (grad_one, grad_two, input_grad)


def solution(mesh):
    return jax.shard_map(
        shards,
        mesh=mesh,
        in_specs=(
            P("feat", "loop"),
            P("loop", "rep", None, None, None),
            P("loop", "rep", None, None),
            P("loop", "rep", None),
            P(),
            P(),
            P(None, ("loop", "feat")),
        ),
        out_specs=(P(), P(), P("feat", "loop")),
        check_vma=False,
    )
```

profile of v0, /device:TPU:8, one launch (start us, length us, event | category | flops | bytes accessed | tf_op | source)
XLA Modules:
  0.0 1272.7 jit_solution(16373129460673330023)
XLA Ops:
  15.7 7.1 collective-permute-done.4
  31.1 51.0 %while.294 = (s32[]{:T(128)}, f32[32,8,128]{2,1,0:T(8,128)S(1)}, s32[]{:T(128)}, s32[]{:T(128)}, s32[112]{0:T(128)S(1)}, /*index=5*/s32[]{:T(128)}, bf16[112,128...) while((s32[]{:T(128)}, f32[32,8,128]{2,1,0:T(8,128)S(1)}, ...), condition=%wide.region_2.3_spmd.clone.clone, body=%wide.region_1.2_spmd.clone.clone.sunk | while | flops 11569371 | bytes 1516121 | solution.py:58
  82.2 106.4 %while.287 = (s32[]{:T(128)}, bf16[32,1024]{1,0:T(8,128)(2,1)S(1)}, f32[32,1024]{1,0:T(8,128)S(1)}, s32[8]{0:T(128)S(1)}, s32[8]{0:T(128)S(1)}, /*index=5*/s32[1...) while((s32[]{:T(128)}, bf16[32,1024]{1,0:T(8,128)(2,1)S(1)}, ...), condition=%wide.region_6.7_spmd, body=%wide.region_3.6_spmd.sunk | while | flops 11602160 | bytes 2565222 | solution.py:83
  90.9 12.7 while.298
  112.8 6.4 while.298
  127.5 6.4 while.298
  142.5 6.9 collective-permute-start.3
  152.6 6.4 while.298
  167.4 6.4 while.298
  182.2 6.4 while.298
  189.4 54.5 %all-reduce.7.cloned.1.call-done = bf16[32,4,256]{2,1,0:T(4,128)(2,1)} async-done(((bf16[32,4,256]{2,1,0:T(4,128)(2,1)}), bf16[32,4,256]{2,1,0:T(4,128)(2,1)}) %all-reduce.7.cloned.1.call-update) | async-done | bytes 65552 | tf_op jit(solution)/shard_map/psum | solution.py:108
  250.3 6.5 all_to_all.109
  274.0 51.0 %while.295 = (s32[]{:T(128)}, f32[32,8,128]{2,1,0:T(8,128)S(1)}, s32[]{:T(128)}, s32[]{:T(128)}, s32[112]{0:T(128)S(1)}, /*index=5*/s32[]{:T(128)}, bf16[112,128...) while((s32[]{:T(128)}, f32[32,8,128]{2,1,0:T(8,128)S(1)}, ...), condition=%wide.region_9.10_spmd.clone.clone, body=%wide.region_8.9_spmd.clone.clone.sunk | while | flops 11569371 | bytes 1516121 | solution.py:58
  325.1 106.4 %while.289 = (s32[]{:T(128)}, bf16[32,1024]{1,0:T(8,128)(2,1)S(1)}, f32[32,1024]{1,0:T(8,128)S(1)}, s32[8]{0:T(128)S(1)}, s32[8]{0:T(128)S(1)}, /*index=5*/s32[1...) while((s32[]{:T(128)}, bf16[32,1024]{1,0:T(8,128)(2,1)S(1)}, ...), condition=%wide.region_13.14_spmd, body=%wide.region_10.13_spmd.sunk | while | flops 11602160 | bytes 2565222 | solution.py:83
  334.0 12.7 while.299
  355.8 6.4 while.299
  370.5 6.4 while.299
  385.4 7.0 collective-permute-start.2
  395.6 6.4 while.299
  410.3 6.4 while.299
  425.1 6.4 while.299
  432.2 57.9 %all-reduce.9.cloned.1.call-done = bf16[32,4,256]{2,1,0:T(4,128)(2,1)} async-done(((bf16[32,4,256]{2,1,0:T(4,128)(2,1)}), bf16[32,4,256]{2,1,0:T(4,128)(2,1)}) %all-reduce.9.cloned.1.call-update) | async-done | bytes 65552 | tf_op jit(solution)/shard_map/psum | solution.py:108
  504.9 6.3 while.296
  511.3 135.5 %while.291 = (s32[]{:T(128)}, bf16[32,1024]{1,0:T(8,128)(2,1)S(1)}, s32[8]{0:T(128)S(1)}, s32[8]{0:T(128)S(1)}, bf16[32,1024]{1,0:T(8,128)(2,1)S(1)}, /*index=5*...) while((s32[]{:T(128)}, bf16[32,1024]{1,0:T(8,128)(2,1)S(1)}, ...), condition=%wide.region_20.21_spmd, body=%wide.region_17.20_spmd.sunk | while | flops 11667697 | bytes 2303082 | solution.py:99
  511.3 6.8 collective-permute-start.1
  520.0 6.3 while.300
  526.4 10.4 collective-permute-start.1
  538.8 6.3 while.300
  559.3 6.3 while.300
  569.6 6.3 while.300
  579.8 12.6 while.300
  596.4 50.3 %while.300 = (s32[]{:T(128)}, f32[32,8,128]{2,1,0:T(8,128)S(1)}, s32[]{:T(128)}, s32[]{:T(128)}, s32[112]{0:T(128)S(1)}, /*index=5*/s32[]{:T(128)}, bf16[112,128...) while((s32[]{:T(128)}, f32[32,8,128]{2,1,0:T(8,128)S(1)}, ...), condition=%wide.region_19.19_spmd.clone.clone, body=%wide.region_18.18_spmd.clone.clone.sunk | while | flops 11569371 | bytes 1516121 | solution.py:58
  648.7 7.7 collective-permute-done.8
  663.3 55.2 %all-reduce.11.cloned.1.call-done = bf16[32,4,256]{2,0,1:T(8,128)(2,1)} async-done(((bf16[32,4,256]{2,0,1:T(8,128)(2,1)}), bf16[32,4,256]{2,0,1:T(8,128)(2,1)}) %all-reduce.11.cloned.1.call-update) | async-done | bytes 65552 | tf_op jit(solution)/shard_map/psum | solution.py:108
  718.6 6.1 all_to_all.111
  733.0 6.3 while.297
  739.4 136.6 %while.293 = (s32[]{:T(128)}, bf16[32,1024]{1,0:T(8,128)(2,1)S(1)}, s32[8]{0:T(128)S(1)}, s32[8]{0:T(128)S(1)}, bf16[32,1024]{1,0:T(8,128)(2,1)S(1)}, /*index=5*...) while((s32[]{:T(128)}, bf16[32,1024]{1,0:T(8,128)(2,1)S(1)}, ...), condition=%wide.region_29.30_spmd, body=%wide.region_26.29_spmd.sunk | while | flops 11667697 | bytes 2303082 | solution.py:99
  739.4 6.8 collective-permute-start
  748.1 6.4 while.301
  754.5 10.4 collective-permute-start
  766.9 6.4 while.301
  787.6 6.4 while.301
  797.9 6.4 while.301
  808.3 12.7 %while.301 = (s32[]{:T(128)}, f32[32,8,128]{2,1,0:T(8,128)S(1)}, s32[]{:T(128)}, s32[]{:T(128)}, s32[112]{0:T(128)S(1)}, /*index=5*/s32[]{:T(128)}, bf16[112,128...) while((s32[]{:T(128)}, f32[32,8,128]{2,1,0:T(8,128)S(1)}, ...), condition=%wide.region_28.28_spmd.clone.clone, body=%wide.region_27.27_spmd.clone.clone.sunk | while | flops 11569371 | bytes 1516121 | solution.py:58
  825.0 51.0 %while.301 = (s32[]{:T(128)}, f32[32,8,128]{2,1,0:T(8,128)S(1)}, s32[]{:T(128)}, s32[]{:T(128)}, s32[112]{0:T(128)S(1)}, /*index=5*/s32[]{:T(128)}, bf16[112,128...) while((s32[]{:T(128)}, f32[32,8,128]{2,1,0:T(8,128)S(1)}, ...), condition=%wide.region_28.28_spmd.clone.clone, body=%wide.region_27.27_spmd.clone.clone.sunk | while | flops 11569371 | bytes 1516121 | solution.py:58
  878.9 7.0 collective-permute-done.10
  892.8 321.2 %all-reduce.15.cloned.1.call-done = (f32[128,128]{1,0:T(8,128)}, f32[128,128]{1,0:T(8,128)}) async-done(((f32[128,128]{1,0:T(8,128)}, f32[128,128]{1,0:T(8,128)}), (f32[128,128]{1,0:T(8,128)}, f32[128,128]{1,0:T(8,128)})) %all-reduce.15.cloned.1.call-update) | async-done | bytes 131088 | tf_op jit(solution)/shard_map/psum | solution.py:118
  1215.5 49.2 %all-reduce.13.cloned.1.call-done = bf16[32,1024]{1,0:T(8,128)(2,1)} async-done(((bf16[32,1024]{1,0:T(8,128)(2,1)}), bf16[32,1024]{1,0:T(8,128)(2,1)}) %all-reduce.13.cloned.1.call-update) | async-done | bytes 65552 | tf_op jit(solution)/shard_map/psum | solution.py:147
  (953 shorter events, 611.6 us)
Async XLA Ops:
  7.2 242.9 %copy-start = (bf16[128,128]{1,0:T(8,128)(2,1)S(1)}, bf16[128,128]{1,0:T(8,128)(2,1)}, u32[]{:S(2)}) copy-start(bf16[128,128]{1,0:T(8,128)(2,1)} %param.35) | copy-start | bytes 98308
  7.2 236.6 %all-reduce.7.cloned.1.call-start = ((), (), s32[]{:S(2)}) async-start(), calls=%async_computation.6 | async-start | bytes 131072 | tf_op jit(solution)/shard_map/psum | solution.py:108
  7.2 15.6 %collective-permute-start.4 = (bf16[32,1024]{1,0:T(8,128)(2,1)}, bf16[32,1024]{1,0:T(8,128)(2,1)S(1)}, u32[]{:S(2)}, u32[]{:S(2)}) collective-permute-start(bf16[32,1024]{1,0:T(8,128)(2,1)} %param.31), channel_id=1, source_target_pairs={{0,16},{16,32},{32,48},{48,64},{64,80},{80,96},{96,112},{112,128},... | collective-permute-start | bytes 196616 | tf_op jit(solution)/shard_map/ppermute | solution.py:13
  23.7 7.4 collective-permute-start.5
  31.1 51.1 %copy-start.2 = (s32[1,1,8]{2,1,0:T(1,128)S(1)}, s32[1,1,8]{2,1,0:T(1,128)}, u32[]{:S(2)}) copy-start(s32[1,1,8]{2,1,0:T(1,128)} %param.34) | copy-start | bytes 100
  82.2 8.7 collective-permute-start.3
  103.7 9.1 collective-permute-start.3
  119.2 8.3 collective-permute-start.3
  134.0 8.4 collective-permute-start.3
  142.5 10.1 collective-permute-start.3
  159.1 8.3 collective-permute-start.3
  173.9 8.3 collective-permute-start.3
  189.3 300.8 %all-reduce.9.cloned.1.call-start = ((), (), s32[]{:S(2)}) async-start(), calls=%async_computation.7 | async-start | bytes 131072 | tf_op jit(solution)/shard_map/psum | solution.py:108
  256.8 9.8 collective-permute-start.6
  266.6 7.4 collective-permute-start.7
  325.1 171.2 %copy-start.1 = (bf16[128,128]{1,0:T(8,128)(2,1)S(1)}, bf16[128,128]{1,0:T(8,128)(2,1)}, u32[]{:S(2)}) copy-start(bf16[128,128]{1,0:T(8,128)(2,1)} %param.36) | copy-start | bytes 98308
  325.1 171.2 %copy-start.3 = (bf16[128,256]{1,0:T(8,128)(2,1)S(1)}, bf16[128,256]{1,0:T(8,128)(2,1)}, u32[]{:S(2)}) copy-start(bf16[128,256]{1,0:T(8,128)(2,1)} %param.37) | copy-start | bytes 196612
  325.1 8.9 collective-permute-start.2
  346.8 8.9 collective-permute-start.2
  362.2 8.3 collective-permute-start.2
  376.9 8.4 collective-permute-start.2
  385.4 10.1 collective-permute-start.2
  402.0 8.3 collective-permute-start.2
  416.8 8.3 collective-permute-start.2
  497.4 7.4 all-to-all-start.3
  502.5 216.1 %all-reduce.11.cloned.1.call-start = ((), (), s32[]{:S(2)}) async-start(), calls=%async_computation.8 | async-start | bytes 131072 | tf_op jit(solution)/shard_map/psum | solution.py:108
  511.3 15.0 %collective-permute-start.1 = (bf16[32,1024]{1,0:T(8,128)(2,1)S(1)}, bf16[32,1024]{1,0:T(8,128)(2,1)S(1)}, u32[]{:S(2)}, u32[]{:S(2)}) collective-permute-start(bf16[32,1024]{1,0:T(8,128)(2,1)S(1)} %get-tuple-element.3920), channel_id=1, source_target_pairs={{0,448},{16,464},{32,480},{48,496},{64,0},{80,16},{96,32},{112,48}... | collective-permute-start | bytes 196616 | tf_op jit(solution)/shard_map/while/body/eval_jaxpr/ppermute | solution.py:13
  526.4 18.7 %collective-permute-start.1 = (bf16[32,1024]{1,0:T(8,128)(2,1)S(1)}, bf16[32,1024]{1,0:T(8,128)(2,1)S(1)}, u32[]{:S(2)}, u32[]{:S(2)}) collective-permute-start(bf16[32,1024]{1,0:T(8,128)(2,1)S(1)} %get-tuple-element.3920), channel_id=1, source_target_pairs={{0,448},{16,464},{32,480},{48,496},{64,0},{80,16},{96,32},{112,48}... | collective-permute-start | bytes 196616 | tf_op jit(solution)/shard_map/while/body/eval_jaxpr/ppermute | solution.py:13
  545.1 7.1 collective-permute-start.1
  552.2 13.4 %collective-permute-start.1 = (bf16[32,1024]{1,0:T(8,128)(2,1)S(1)}, bf16[32,1024]{1,0:T(8,128)(2,1)S(1)}, u32[]{:S(2)}, u32[]{:S(2)}) collective-permute-start(bf16[32,1024]{1,0:T(8,128)(2,1)S(1)} %get-tuple-element.3920), channel_id=1, source_target_pairs={{0,448},{16,464},{32,480},{48,496},{64,0},{80,16},{96,32},{112,48}... | collective-permute-start | bytes 196616 | tf_op jit(solution)/shard_map/while/body/eval_jaxpr/ppermute | solution.py:13
  565.6 10.2 collective-permute-start.1
  575.9 16.5 %collective-permute-start.1 = (bf16[32,1024]{1,0:T(8,128)(2,1)S(1)}, bf16[32,1024]{1,0:T(8,128)(2,1)S(1)}, u32[]{:S(2)}, u32[]{:S(2)}) collective-permute-start(bf16[32,1024]{1,0:T(8,128)(2,1)S(1)} %get-tuple-element.3920), channel_id=1, source_target_pairs={{0,448},{16,464},{32,480},{48,496},{64,0},{80,16},{96,32},{112,48}... | collective-permute-start | bytes 196616 | tf_op jit(solution)/shard_map/while/body/eval_jaxpr/ppermute | solution.py:13
  592.5 54.2 %collective-permute-start.1 = (bf16[32,1024]{1,0:T(8,128)(2,1)S(1)}, bf16[32,1024]{1,0:T(8,128)(2,1)S(1)}, u32[]{:S(2)}, u32[]{:S(2)}) collective-permute-start(bf16[32,1024]{1,0:T(8,128)(2,1)S(1)} %get-tuple-element.3920), channel_id=1, source_target_pairs={{0,448},{16,464},{32,480},{48,496},{64,0},{80,16},{96,32},{112,48}... | collective-permute-start | bytes 196616 | tf_op jit(solution)/shard_map/while/body/eval_jaxpr/ppermute | solution.py:13
  646.7 9.7 collective-permute-start.8
  656.5 6.2 collective-permute-start.9
  725.5 7.4 all-to-all-start.5
  730.6 483.4 %all-reduce.15.cloned.1.call-start = ((), (), s32[]{:S(2)}) async-start(), calls=%async_computation.10 | async-start | bytes 262144 | tf_op jit(solution)/shard_map/psum | solution.py:118
  739.4 15.1 %collective-permute-start = (bf16[32,1024]{1,0:T(8,128)(2,1)S(1)}, bf16[32,1024]{1,0:T(8,128)(2,1)S(1)}, u32[]{:S(2)}, u32[]{:S(2)}) collective-permute-start(bf16[32,1024]{1,0:T(8,128)(2,1)S(1)} %get-tuple-element.4004), channel_id=1, source_target_pairs={{0,448},{16,464},{32,480},{48,496},{64,0},{80,16},{96,32},{112,48}... | collective-permute-start | bytes 196616 | tf_op jit(solution)/shard_map/while/body/eval_jaxpr/ppermute | solution.py:13
  754.5 18.8 %collective-permute-start = (bf16[32,1024]{1,0:T(8,128)(2,1)S(1)}, bf16[32,1024]{1,0:T(8,128)(2,1)S(1)}, u32[]{:S(2)}, u32[]{:S(2)}) collective-permute-start(bf16[32,1024]{1,0:T(8,128)(2,1)S(1)} %get-tuple-element.4004), channel_id=1, source_target_pairs={{0,448},{16,464},{32,480},{48,496},{64,0},{80,16},{96,32},{112,48}... | collective-permute-start | bytes 196616 | tf_op jit(solution)/shard_map/while/body/eval_jaxpr/ppermute | solution.py:13
  773.4 7.1 collective-permute-start
  780.5 13.5 %collective-permute-start = (bf16[32,1024]{1,0:T(8,128)(2,1)S(1)}, bf16[32,1024]{1,0:T(8,128)(2,1)S(1)}, u32[]{:S(2)}, u32[]{:S(2)}) collective-permute-start(bf16[32,1024]{1,0:T(8,128)(2,1)S(1)} %get-tuple-element.4004), channel_id=1, source_target_pairs={{0,448},{16,464},{32,480},{48,496},{64,0},{80,16},{96,32},{112,48}... | collective-permute-start | bytes 196616 | tf_op jit(solution)/shard_map/while/body/eval_jaxpr/ppermute | solution.py:13
  794.0 10.3 collective-permute-start
  804.4 16.6 %collective-permute-start = (bf16[32,1024]{1,0:T(8,128)(2,1)S(1)}, bf16[32,1024]{1,0:T(8,128)(2,1)S(1)}, u32[]{:S(2)}, u32[]{:S(2)}) collective-permute-start(bf16[32,1024]{1,0:T(8,128)(2,1)S(1)} %get-tuple-element.4004), channel_id=1, source_target_pairs={{0,448},{16,464},{32,480},{48,496},{64,0},{80,16},{96,32},{112,48}... | collective-permute-start | bytes 196616 | tf_op jit(solution)/shard_map/while/body/eval_jaxpr/ppermute | solution.py:13
  821.1 54.9 %collective-permute-start = (bf16[32,1024]{1,0:T(8,128)(2,1)S(1)}, bf16[32,1024]{1,0:T(8,128)(2,1)S(1)}, u32[]{:S(2)}, u32[]{:S(2)}) collective-permute-start(bf16[32,1024]{1,0:T(8,128)(2,1)S(1)} %get-tuple-element.4004), channel_id=1, source_target_pairs={{0,448},{16,464},{32,480},{48,496},{64,0},{80,16},{96,32},{112,48}... | collective-permute-start | bytes 196616 | tf_op jit(solution)/shard_map/while/body/eval_jaxpr/ppermute | solution.py:13
  876.0 9.9 collective-permute-start.10
  885.9 6.2 collective-permute-start.11
  888.7 376.0 %all-reduce.13.cloned.1.call-start = ((), (), s32[]{:S(2)}) async-start(), calls=%async_computation.9 | async-start | bytes 131072 | tf_op jit(solution)/shard_map/psum | solution.py:147
Sparse Core Ops, SparseCore 0:
  189.4 54.3 all-reduce.6
  432.4 57.7 all-reduce.8
  663.5 55.0 all-reduce.10
  888.8 325.1 all-reduce.14
  1216.1 48.5 all-reduce.12
where the time goes:
time: 1280 us; the launch traced here: 1270 us
  waiting for transfers between devices  650 us (51%)
  local copies, waits for them, and re-layouts  314 us (25%)
  starting transfers between devices  129 us (10%)
  other arithmetic  84 us (7%)
  matrix products  32.4 us (3%)
  loops' own time  25.1 us (2%)
  blocking collectives  23.3 us (2%)
  between operations  15.5 us (1%)
    psum x1, waiting for transfers between devices, weight_grad(): return lax.psum(part_sum, ('loop', 'feat'))  321 us
    psum x3, waiting for transfers between devices, to_nodes(): summed = lax.psum(partial_value.astype(jnp.bfloat16), 'rep')  168 us
    gather x60, local copies, waits for them, and re-layouts, one_round(): chosen = tile_set[slot_ids]  158 us
    ppermute x36, starting transfers between devices, passed_along(): return lax.ppermute(value, axis, pairs)  119 us
    ppermute x36, waiting for transfers between devices, passed_along(): return lax.ppermute(value, axis, pairs)  108 us
    psum x1, waiting for transfers between devices, shards(): input_grad = lax.psum(partial_value.astype(jnp.bfloat16), 'rep')  49.2 us
    lt x60, other arithmetic, one_round(): alive_mask = within < number  40 us
    gather x60, local copies, waits for them, and re-layouts, one_round(): picked = shaped[:, row_ids[slot_ids], :]  36.2 us
  transfers between devices with their start and end apart: 43, of which 31 were waited for; matrix products, arithmetic and copies ran while one was open for 17% of the time, Pallas kernels for 0%

commit v1 on v0

--- a/solution.py
+++ b/solution.py
@@ -115,7 +115,7 @@
 
 def weight_grad(mixed, slope):
     part_sum = jnp.einsum("dq,eq->de", mixed, slope, preferred_element_type=jnp.float32)
-    return lax.psum(part_sum, ("loop", "feat"))
+    return jnp.sum(lax.all_gather(part_sum, ("loop", "feat")), axis=0)
 
 
 def shards(features, tile_values, tile_coords, section_counts, weight_one, weight_two, cotangent):

time: 1280 us -> 1080 us (0.84)
  waiting for transfers between devices: 650 us -> 450 us
    psum x1 -> x0, waiting for transfers between devices: 321 us -> none  [weight_grad(): return lax.psum(part_sum, ('loop', 'feat'))]
    all_gather x0 -> x2, waiting for transfers between devices: none -> 118 us  [weight_grad(): return jnp.sum(lax.all_gather(part_sum, ('loop', 'feat')), axis=0)]
  transfers between devices with their start and end apart: 43 -> 45, of which waited for: 31 -> 32; matrix products, arithmetic and copies ran while one was open for 17% -> 22% of each run, Pallas kernels for 0% -> 0%
where the time goes in v1:
time: 1080 us
  waiting for transfers between devices  450 us (42%)
  local copies, waits for them, and re-layouts  314 us (29%)
  starting transfers between devices  134 us (12%)
  other arithmetic  91.8 us (8%)
  matrix products  32.4 us (3%)
  loops' own time  24.1 us (2%)
  blocking collectives  17.2 us (2%)
  between operations  15.9 us (1%)
    psum x3, waiting for transfers between devices, to_nodes(): summed = lax.psum(partial_value.astype(jnp.bfloat16), 'rep')  167 us
    gather x60, local copies, waits for them, and re-layouts, one_round(): chosen = tile_set[slot_ids]  159 us
    ppermute x36, starting transfers between devices, passed_along(): return lax.ppermute(value, axis, pairs)  120 us
    all_gather x2, waiting for transfers between devices, weight_grad(): return jnp.sum(lax.all_gather(part_sum, ('loop', 'feat')), axis=0)  118 us
    ppermute x36, waiting for transfers between devices, passed_along(): return lax.ppermute(value, axis, pairs)  110 us
    psum x1, waiting for transfers between devices, shards(): input_grad = lax.psum(partial_value.astype(jnp.bfloat16), 'rep')  50.3 us
    lt x60, other arithmetic, one_round(): alive_mask = within < number  39.3 us
    gather x60, local copies, waits for them, and re-layouts, one_round(): picked = shaped[:, row_ids[slot_ids], :]  36.2 us
  transfers between devices with their start and end apart: 45, of which 32 were waited for; matrix products, arithmetic and copies ran while one was open for 22% of the time, Pallas kernels for 0%

profile of v1, /device:TPU:8, one launch (start us, length us, event | category | flops | bytes accessed | tf_op | source)
XLA Modules:
  0.0 1079.1 jit_solution(16261774855965846544)
XLA Ops:
  15.8 7.0 collective-permute-done.4
  31.1 51.0 %while.294 = (s32[]{:T(128)}, f32[32,8,128]{2,1,0:T(8,128)S(1)}, s32[]{:T(128)}, s32[]{:T(128)}, s32[112]{0:T(128)S(1)}, /*index=5*/s32[]{:T(128)}, bf16[112,128...) while((s32[]{:T(128)}, f32[32,8,128]{2,1,0:T(8,128)S(1)}, ...), condition=%wide.region_2.3_spmd.clone.clone, body=%wide.region_1.2_spmd.clone.clone.sunk | while | flops 11569371 | bytes 1516121 | solution.py:58
  82.2 106.4 %while.287 = (s32[]{:T(128)}, bf16[32,1024]{1,0:T(8,128)(2,1)S(1)}, f32[32,1024]{1,0:T(8,128)S(1)}, s32[8]{0:T(128)S(1)}, s32[8]{0:T(128)S(1)}, /*index=5*/s32[1...) while((s32[]{:T(128)}, bf16[32,1024]{1,0:T(8,128)(2,1)S(1)}, ...), condition=%wide.region_6.7_spmd, body=%wide.region_3.6_spmd.sunk | while | flops 11602160 | bytes 2565222 | solution.py:83
  90.9 12.7 %while.298 = (s32[]{:T(128)}, f32[32,8,128]{2,1,0:T(8,128)S(1)}, s32[]{:T(128)}, s32[]{:T(128)}, s32[112]{0:T(128)S(1)}, /*index=5*/s32[]{:T(128)}, bf16[112,128...) while((s32[]{:T(128)}, f32[32,8,128]{2,1,0:T(8,128)S(1)}, ...), condition=%wide.region_5.5_spmd.clone.clone, body=%wide.region_4.4_spmd.clone.clone.sunk | while | flops 11569371 | bytes 1516121 | solution.py:58
  112.8 6.4 while.298
  127.5 6.4 while.298
  142.4 7.8 collective-permute-start.3
  152.6 6.4 while.298
  167.4 6.4 while.298
  182.1 6.4 while.298
  189.3 54.5 %all-reduce.5.cloned.1.call-done = bf16[32,4,256]{2,1,0:T(4,128)(2,1)} async-done(((bf16[32,4,256]{2,1,0:T(4,128)(2,1)}), bf16[32,4,256]{2,1,0:T(4,128)(2,1)}) %all-reduce.5.cloned.1.call-update) | async-done | bytes 65552 | tf_op jit(solution)/shard_map/psum | solution.py:108
  250.3 6.5 all_to_all.109
  260.9 5.7 collective-permute-done.6
  274.0 51.0 %while.295 = (s32[]{:T(128)}, f32[32,8,128]{2,1,0:T(8,128)S(1)}, s32[]{:T(128)}, s32[]{:T(128)}, s32[112]{0:T(128)S(1)}, /*index=5*/s32[]{:T(128)}, bf16[112,128...) while((s32[]{:T(128)}, f32[32,8,128]{2,1,0:T(8,128)S(1)}, ...), condition=%wide.region_9.10_spmd.clone.clone, body=%wide.region_8.9_spmd.clone.clone.sunk | while | flops 11569371 | bytes 1516121 | solution.py:58
  325.1 107.0 %while.289 = (s32[]{:T(128)}, bf16[32,1024]{1,0:T(8,128)(2,1)S(1)}, f32[32,1024]{1,0:T(8,128)S(1)}, s32[8]{0:T(128)S(1)}, s32[8]{0:T(128)S(1)}, /*index=5*/s32[1...) while((s32[]{:T(128)}, bf16[32,1024]{1,0:T(8,128)(2,1)S(1)}, ...), condition=%wide.region_13.14_spmd, body=%wide.region_10.13_spmd.sunk | while | flops 11602160 | bytes 2565222 | solution.py:83
  334.1 12.9 %while.299 = (s32[]{:T(128)}, f32[32,8,128]{2,1,0:T(8,128)S(1)}, s32[]{:T(128)}, s32[]{:T(128)}, s32[112]{0:T(128)S(1)}, /*index=5*/s32[]{:T(128)}, bf16[112,128...) while((s32[]{:T(128)}, f32[32,8,128]{2,1,0:T(8,128)S(1)}, ...), condition=%wide.region_12.12_spmd.clone.clone, body=%wide.region_11.11_spmd.clone.clone.sunk | while | flops 11569371 | bytes 1516121 | solution.py:58
  355.9 6.4 while.299
  370.8 6.4 while.299
  385.8 7.0 collective-permute-start.2
  396.0 6.4 while.299
  410.8 6.4 while.299
  425.7 6.4 while.299
  432.9 58.0 %all-reduce.7.cloned.1.call-done = bf16[32,4,256]{2,1,0:T(4,128)(2,1)} async-done(((bf16[32,4,256]{2,1,0:T(4,128)(2,1)}), bf16[32,4,256]{2,1,0:T(4,128)(2,1)}) %all-reduce.7.cloned.1.call-update) | async-done | bytes 65552 | tf_op jit(solution)/shard_map/psum | solution.py:108
  505.6 6.3 while.296
  512.0 136.5 %while.291 = (s32[]{:T(128)}, bf16[32,1024]{1,0:T(8,128)(2,1)S(1)}, s32[8]{0:T(128)S(1)}, s32[8]{0:T(128)S(1)}, bf16[32,1024]{1,0:T(8,128)(2,1)S(1)}, /*index=5*...) while((s32[]{:T(128)}, bf16[32,1024]{1,0:T(8,128)(2,1)S(1)}, ...), condition=%wide.region_20.21_spmd, body=%wide.region_17.20_spmd.sunk | while | flops 11667697 | bytes 2303082 | solution.py:99
  512.0 6.8 collective-permute-start.1
  520.7 6.4 while.300
  527.1 10.4 collective-permute-start.1
  539.5 6.4 while.300
  560.1 6.4 while.300
  570.4 6.4 while.300
  580.8 12.7 %while.300 = (s32[]{:T(128)}, f32[32,8,128]{2,1,0:T(8,128)S(1)}, s32[]{:T(128)}, s32[]{:T(128)}, s32[112]{0:T(128)S(1)}, /*index=5*/s32[]{:T(128)}, bf16[112,128...) while((s32[]{:T(128)}, f32[32,8,128]{2,1,0:T(8,128)S(1)}, ...), condition=%wide.region_19.19_spmd.clone.clone, body=%wide.region_18.18_spmd.clone.clone.sunk | while | flops 11569371 | bytes 1516121 | solution.py:58
  597.5 50.9 %while.300 = (s32[]{:T(128)}, f32[32,8,128]{2,1,0:T(8,128)S(1)}, s32[]{:T(128)}, s32[]{:T(128)}, s32[112]{0:T(128)S(1)}, /*index=5*/s32[]{:T(128)}, bf16[112,128...) while((s32[]{:T(128)}, f32[32,8,128]{2,1,0:T(8,128)S(1)}, ...), condition=%wide.region_19.19_spmd.clone.clone, body=%wide.region_18.18_spmd.clone.clone.sunk | while | flops 11569371 | bytes 1516121 | solution.py:58
  650.4 7.8 collective-permute-done.8
  665.9 54.3 %all-reduce.9.cloned.1.call-done = bf16[32,4,256]{2,0,1:T(8,128)(2,1)} async-done(((bf16[32,4,256]{2,0,1:T(8,128)(2,1)}), bf16[32,4,256]{2,0,1:T(8,128)(2,1)}) %all-reduce.9.cloned.1.call-update) | async-done | bytes 65552 | tf_op jit(solution)/shard_map/psum | solution.py:108
  734.7 6.3 while.297
  741.0 135.8 %while.293 = (s32[]{:T(128)}, bf16[32,1024]{1,0:T(8,128)(2,1)S(1)}, s32[8]{0:T(128)S(1)}, s32[8]{0:T(128)S(1)}, bf16[32,1024]{1,0:T(8,128)(2,1)S(1)}, /*index=5*...) while((s32[]{:T(128)}, bf16[32,1024]{1,0:T(8,128)(2,1)S(1)}, ...), condition=%wide.region_29.30_spmd, body=%wide.region_26.29_spmd.sunk | while | flops 11667697 | bytes 2303082 | solution.py:99
  741.0 6.8 collective-permute-start
  749.8 6.3 while.301
  756.1 10.4 collective-permute-start
  768.5 6.3 while.301
  789.1 6.3 while.301
  799.3 6.3 while.301
  809.6 12.6 %while.301 = (s32[]{:T(128)}, f32[32,8,128]{2,1,0:T(8,128)S(1)}, s32[]{:T(128)}, s32[]{:T(128)}, s32[112]{0:T(128)S(1)}, /*index=5*/s32[]{:T(128)}, bf16[112,128...) while((s32[]{:T(128)}, f32[32,8,128]{2,1,0:T(8,128)S(1)}, ...), condition=%wide.region_28.28_spmd.clone.clone, body=%wide.region_27.27_spmd.clone.clone.sunk | while | flops 11569371 | bytes 1516121 | solution.py:58
  826.2 50.6 %while.301 = (s32[]{:T(128)}, f32[32,8,128]{2,1,0:T(8,128)S(1)}, s32[]{:T(128)}, s32[]{:T(128)}, s32[112]{0:T(128)S(1)}, /*index=5*/s32[]{:T(128)}, bf16[112,128...) while((s32[]{:T(128)}, f32[32,8,128]{2,1,0:T(8,128)S(1)}, ...), condition=%wide.region_28.28_spmd.clone.clone, body=%wide.region_27.27_spmd.clone.clone.sunk | while | flops 11569371 | bytes 1516121 | solution.py:58
  879.2 7.8 collective-permute-done.10
  898.5 117.6 %all-gather.5.cloned.1.call-done = f32[16384,128]{1,0:T(8,128)} async-done(((f32[128,128]{1,0:T(8,128)}), f32[16384,128]{1,0:T(8,128)}) %all-gather.5.cloned.1.call-update) | async-done | bytes 8388624 | tf_op jit(solution)/shard_map/all_gather | solution.py:118
  1020.5 50.3 %all-reduce.11.cloned.1.call-done = bf16[32,1024]{1,0:T(8,128)(2,1)} async-done(((bf16[32,1024]{1,0:T(8,128)(2,1)}), bf16[32,1024]{1,0:T(8,128)(2,1)}) %all-reduce.11.cloned.1.call-update) | async-done | bytes 65552 | tf_op jit(solution)/shard_map/psum | solution.py:147
  (960 shorter events, 620.6 us)
Async XLA Ops:
  7.2 242.9 %copy-start = (bf16[128,128]{1,0:T(8,128)(2,1)S(1)}, bf16[128,128]{1,0:T(8,128)(2,1)}, u32[]{:S(2)}) copy-start(bf16[128,128]{1,0:T(8,128)(2,1)} %param.35) | copy-start | bytes 98308
  7.2 236.6 %all-reduce.5.cloned.1.call-start = ((), (), s32[]{:S(2)}) async-start(), calls=%async_computation.6 | async-start | bytes 131072 | tf_op jit(solution)/shard_map/psum | solution.py:108
  7.2 15.6 %collective-permute-start.4 = (bf16[32,1024]{1,0:T(8,128)(2,1)}, bf16[32,1024]{1,0:T(8,128)(2,1)S(1)}, u32[]{:S(2)}, u32[]{:S(2)}) collective-permute-start(bf16[32,1024]{1,0:T(8,128)(2,1)} %param.31), channel_id=1, source_target_pairs={{0,16},{16,32},{32,48},{48,64},{64,80},{80,96},{96,112},{112,128},... | collective-permute-start | bytes 196616 | tf_op jit(solution)/shard_map/ppermute | solution.py:13
  23.7 7.4 collective-permute-start.5
  82.2 8.7 collective-permute-start.3
  103.7 9.1 collective-permute-start.3
  119.2 8.3 collective-permute-start.3
  134.0 8.3 collective-permute-start.3
  142.4 10.2 collective-permute-start.3
  159.0 8.3 collective-permute-start.3
  173.8 8.3 collective-permute-start.3
  189.3 301.6 %all-reduce.7.cloned.1.call-start = ((), (), s32[]{:S(2)}) async-start(), calls=%async_computation.7 | async-start | bytes 131072 | tf_op jit(solution)/shard_map/psum | solution.py:108
  256.8 9.8 collective-permute-start.6
  266.6 7.4 collective-permute-start.7
  325.1 171.9 %copy-start.1 = (bf16[128,128]{1,0:T(8,128)(2,1)S(1)}, bf16[128,128]{1,0:T(8,128)(2,1)}, u32[]{:S(2)}) copy-start(bf16[128,128]{1,0:T(8,128)(2,1)} %param.36) | copy-start | bytes 98308
  325.1 171.9 %copy-start.3 = (bf16[128,256]{1,0:T(8,128)(2,1)S(1)}, bf16[128,256]{1,0:T(8,128)(2,1)}, u32[]{:S(2)}) copy-start(bf16[128,256]{1,0:T(8,128)(2,1)} %param.37) | copy-start | bytes 196612
  325.2 8.9 collective-permute-start.2
  347.0 8.9 collective-permute-start.2
  362.5 8.3 collective-permute-start.2
  377.3 8.4 collective-permute-start.2
  385.8 10.2 collective-permute-start.2
  402.5 8.3 collective-permute-start.2
  417.3 8.3 collective-permute-start.2
  498.1 7.4 all-to-all-start.3
  503.2 217.1 %all-reduce.9.cloned.1.call-start = ((), (), s32[]{:S(2)}) async-start(), calls=%async_computation.8 | async-start | bytes 131072 | tf_op jit(solution)/shard_map/psum | solution.py:108
  512.0 15.1 %collective-permute-start.1 = (bf16[32,1024]{1,0:T(8,128)(2,1)S(1)}, bf16[32,1024]{1,0:T(8,128)(2,1)S(1)}, u32[]{:S(2)}, u32[]{:S(2)}) collective-permute-start(bf16[32,1024]{1,0:T(8,128)(2,1)S(1)} %get-tuple-element.3916), channel_id=1, source_target_pairs={{0,448},{16,464},{32,480},{48,496},{64,0},{80,16},{96,32},{112,48}... | collective-permute-start | bytes 196616 | tf_op jit(solution)/shard_map/while/body/eval_jaxpr/ppermute | solution.py:13
  527.1 18.7 %collective-permute-start.1 = (bf16[32,1024]{1,0:T(8,128)(2,1)S(1)}, bf16[32,1024]{1,0:T(8,128)(2,1)S(1)}, u32[]{:S(2)}, u32[]{:S(2)}) collective-permute-start(bf16[32,1024]{1,0:T(8,128)(2,1)S(1)} %get-tuple-element.3916), channel_id=1, source_target_pairs={{0,448},{16,464},{32,480},{48,496},{64,0},{80,16},{96,32},{112,48}... | collective-permute-start | bytes 196616 | tf_op jit(solution)/shard_map/while/body/eval_jaxpr/ppermute | solution.py:13
  545.9 7.1 collective-permute-start.1
  553.0 13.5 %collective-permute-start.1 = (bf16[32,1024]{1,0:T(8,128)(2,1)S(1)}, bf16[32,1024]{1,0:T(8,128)(2,1)S(1)}, u32[]{:S(2)}, u32[]{:S(2)}) collective-permute-start(bf16[32,1024]{1,0:T(8,128)(2,1)S(1)} %get-tuple-element.3916), channel_id=1, source_target_pairs={{0,448},{16,464},{32,480},{48,496},{64,0},{80,16},{96,32},{112,48}... | collective-permute-start | bytes 196616 | tf_op jit(solution)/shard_map/while/body/eval_jaxpr/ppermute | solution.py:13
  566.6 10.3 collective-permute-start.1
  576.9 16.6 %collective-permute-start.1 = (bf16[32,1024]{1,0:T(8,128)(2,1)S(1)}, bf16[32,1024]{1,0:T(8,128)(2,1)S(1)}, u32[]{:S(2)}, u32[]{:S(2)}) collective-permute-start(bf16[32,1024]{1,0:T(8,128)(2,1)S(1)} %get-tuple-element.3916), channel_id=1, source_target_pairs={{0,448},{16,464},{32,480},{48,496},{64,0},{80,16},{96,32},{112,48}... | collective-permute-start | bytes 196616 | tf_op jit(solution)/shard_map/while/body/eval_jaxpr/ppermute | solution.py:13
  593.6 54.8 %collective-permute-start.1 = (bf16[32,1024]{1,0:T(8,128)(2,1)S(1)}, bf16[32,1024]{1,0:T(8,128)(2,1)S(1)}, u32[]{:S(2)}, u32[]{:S(2)}) collective-permute-start(bf16[32,1024]{1,0:T(8,128)(2,1)S(1)} %get-tuple-element.3916), channel_id=1, source_target_pairs={{0,448},{16,464},{32,480},{48,496},{64,0},{80,16},{96,32},{112,48}... | collective-permute-start | bytes 196616 | tf_op jit(solution)/shard_map/while/body/eval_jaxpr/ppermute | solution.py:13
  648.5 9.7 collective-permute-start.8
  658.2 6.2 collective-permute-start.9
  665.1 228.9 %all-gather.7.cloned.1.call-start = ((), (), s32[]{:S(2)}) async-start(), calls=%async_computation.11 | async-start | bytes 8454144 | tf_op jit(solution)/shard_map/all_gather | solution.py:118
  720.3 6.1 all-to-all-start.4
  727.2 7.4 all-to-all-start.5
  732.3 283.8 %all-gather.5.cloned.1.call-start = ((), (), s32[]{:S(2)}) async-start(), calls=%async_computation.10 | async-start | bytes 8454144 | tf_op jit(solution)/shard_map/all_gather | solution.py:118
  733.1 337.7 %all-reduce.11.cloned.1.call-start = ((), (), s32[]{:S(2)}) async-start(), calls=%async_computation.9 | async-start | bytes 131072 | tf_op jit(solution)/shard_map/psum | solution.py:147
  741.0 15.0 %collective-permute-start = (bf16[32,1024]{1,0:T(8,128)(2,1)S(1)}, bf16[32,1024]{1,0:T(8,128)(2,1)S(1)}, u32[]{:S(2)}, u32[]{:S(2)}) collective-permute-start(bf16[32,1024]{1,0:T(8,128)(2,1)S(1)} %get-tuple-element.4000), channel_id=1, source_target_pairs={{0,448},{16,464},{32,480},{48,496},{64,0},{80,16},{96,32},{112,48}... | collective-permute-start | bytes 196616 | tf_op jit(solution)/shard_map/while/body/eval_jaxpr/ppermute | solution.py:13
  756.1 18.7 %collective-permute-start = (bf16[32,1024]{1,0:T(8,128)(2,1)S(1)}, bf16[32,1024]{1,0:T(8,128)(2,1)S(1)}, u32[]{:S(2)}, u32[]{:S(2)}) collective-permute-start(bf16[32,1024]{1,0:T(8,128)(2,1)S(1)} %get-tuple-element.4000), channel_id=1, source_target_pairs={{0,448},{16,464},{32,480},{48,496},{64,0},{80,16},{96,32},{112,48}... | collective-permute-start | bytes 196616 | tf_op jit(solution)/shard_map/while/body/eval_jaxpr/ppermute | solution.py:13
  774.9 7.2 collective-permute-start
  782.1 13.3 %collective-permute-start = (bf16[32,1024]{1,0:T(8,128)(2,1)S(1)}, bf16[32,1024]{1,0:T(8,128)(2,1)S(1)}, u32[]{:S(2)}, u32[]{:S(2)}) collective-permute-start(bf16[32,1024]{1,0:T(8,128)(2,1)S(1)} %get-tuple-element.4000), channel_id=1, source_target_pairs={{0,448},{16,464},{32,480},{48,496},{64,0},{80,16},{96,32},{112,48}... | collective-permute-start | bytes 196616 | tf_op jit(solution)/shard_map/while/body/eval_jaxpr/ppermute | solution.py:13
  795.4 10.2 collective-permute-start
  805.7 16.5 %collective-permute-start = (bf16[32,1024]{1,0:T(8,128)(2,1)S(1)}, bf16[32,1024]{1,0:T(8,128)(2,1)S(1)}, u32[]{:S(2)}, u32[]{:S(2)}) collective-permute-start(bf16[32,1024]{1,0:T(8,128)(2,1)S(1)} %get-tuple-element.4000), channel_id=1, source_target_pairs={{0,448},{16,464},{32,480},{48,496},{64,0},{80,16},{96,32},{112,48}... | collective-permute-start | bytes 196616 | tf_op jit(solution)/shard_map/while/body/eval_jaxpr/ppermute | solution.py:13
  822.3 54.5 %collective-permute-start = (bf16[32,1024]{1,0:T(8,128)(2,1)S(1)}, bf16[32,1024]{1,0:T(8,128)(2,1)S(1)}, u32[]{:S(2)}, u32[]{:S(2)}) collective-permute-start(bf16[32,1024]{1,0:T(8,128)(2,1)S(1)} %get-tuple-element.4000), channel_id=1, source_target_pairs={{0,448},{16,464},{32,480},{48,496},{64,0},{80,16},{96,32},{112,48}... | collective-permute-start | bytes 196616 | tf_op jit(solution)/shard_map/while/body/eval_jaxpr/ppermute | solution.py:13
  876.9 10.2 collective-permute-start.10
  887.1 6.2 collective-permute-start.11
  (1 other events, 51.1 us)
Sparse Core Ops, SparseCore 0:
  189.4 54.3 all-reduce.4
  433.0 57.7 all-reduce.6
  665.2 55.0 all-reduce.8
  723.8 145.8 all-gather.6
  873.3 142.7 all-gather.4
  1018.2 52.5 all-reduce.10
